TPU v7x, 32 devices: a whole 2x2x4 slice. The times are simulated.
32 devices in a mesh: row: 4 (over y, core), col: 8 (over z, x).
Axes of the slice: x: 2, y: 2, z: 4, core: 2. Of those that a mesh axis runs over, the one named last changes fastest.
Arguments:
- records: bfloat16 [16, 8192, 4096], P('col', 'row'), may hold values from -6 to 6
- centre_bins: int32 [2], replicated, may hold values from 33 to 2016, as said below
- segment_valid: int32 [16], replicated, may hold values 0 or 1
Outputs:
- coherency: float32 [2, 2, 8192, 8192], P(None, None, 'row', 'col')
Inputs may be any that keep to these rules, and one draw needn't show every extreme that they name: `centre_bins`: the selected bins are all different and one of them is the highest allowed; their bands may intersect.
All inputs are finite; a program needn't handle non-finite values.
Results may differ from a plain program's by a relative error of at most 0.0049.
Values may be sent and summed in bfloat16 or wider, within the bound.
No kernel may reach another device: no remote copies, remote signals or barrier semaphores. Data moves between devices by JAX's collectives and lax.ppermute only.
A program may use at most 256 MiB of HBM per device.

v0:
```python
import math

import jax
import jax.numpy as jnp
from jax import lax
from jax.sharding import PartitionSpec as P

BAND = 64
NSEL = 2


def from_root(block, axis, source):
    block = jnp.where(lax.axis_index(axis) == source, block, jnp.zeros_like(block))
    return lax.psum(block, axis)


def transform_table(centre_bins, length):
    samples = lax.broadcasted_iota(jnp.int32, (length, 1, 1), 0)
    offsets = jnp.arange(BAND, dtype=jnp.int32) - BAND // 2
    frequencies = centre_bins[:, None] + offsets[None, :]
    phases = samples * frequencies[None, :, :] % length
    angles = phases.astype(jnp.float32) * (2.0 * math.pi / length)
    factor = 1.0 / math.sqrt(length)
    stacked = jnp.stack([jnp.cos(angles) * factor, -jnp.sin(angles) * factor], axis=2)
    return stacked.reshape(length, NSEL * 2 * BAND).astype(jnp.bfloat16)


def whiten(spectra):
    grouped = spectra.reshape(spectra.shape[0], NSEL, 2, BAND)
    real_part = grouped[:, :, 0, :]
    imag_part = grouped[:, :, 1, :]
    amplitude = jnp.mean(jnp.sqrt(real_part * real_part + imag_part * imag_part), axis=2)
    scaled = grouped / (amplitude[:, :, None, None] + 1e-06)
    return scaled.reshape(spectra.shape[0], NSEL * 2 * BAND).astype(jnp.bfloat16)


def prepare_right(right_side):
    prepared = []
    for band_index in range(NSEL):
        bin_block = right_side[:, :, band_index * 2 * BAND : (band_index + 1) * 2 * BAND]
        turned = jnp.concatenate([-bin_block[:, :, BAND:], bin_block[:, :, :BAND]], axis=2)
        prepared.append(jnp.concatenate([bin_block, turned], axis=1))
    return jnp.stack(prepared, axis=0)


def pair_terms(left_side, prepared):
    half_width = prepared.shape[2] // 2
    results = []
    for band_index in range(NSEL):
        bin_block = left_side[:, :, band_index * 2 * BAND : (band_index + 1) * 2 * BAND]
        product = lax.dot_general(
            bin_block,
            prepared[band_index],
            (((0, 2), (0, 2)), ((), ())),
            preferred_element_type=jnp.float32,
        )
        results.append(jnp.stack([product[:, :half_width], product[:, half_width:]], axis=0))
    return jnp.stack(results, axis=0)


def shards(records, centre_bins, segment_valid):
    seg_count, row_count, length = records.shape
    weights = transform_table(centre_bins, length)
    spectra = jnp.dot(
        records.reshape(seg_count * row_count, length), weights, preferred_element_type=jnp.float32
    )
    whitened = whiten(spectra).reshape(seg_count, row_count, NSEL * 2 * BAND)
    valid_weight = segment_valid.astype(jnp.bfloat16)
    factor = 1.0 / (segment_valid.shape[0] * BAND)
    row_side = lax.all_gather(whitened, "col", axis=0, tiled=True)
    block_ratio = lax.axis_size("col") // lax.axis_size("row")
    col_count = row_count // block_ratio
    column_index = lax.axis_index("col")
    offset = column_index % block_ratio * col_count
    local_part = lax.dynamic_slice_in_dim(row_side, offset, col_count, 1)
    column_side = from_root(local_part, "row", column_index // block_ratio)
    summed = pair_terms(row_side * valid_weight[:, None, None], prepare_right(column_side))
    return summed * factor


def solution(mesh):
    placed = (P("col", "row", None), P(), P())
    return jax.shard_map(
        shards, mesh=mesh, in_specs=placed, out_specs=P(None, None, "row", "col"), check_vma=False
    )
```

profile of v0, /device:TPU:0, one launch (start us, length us, event | category | flops | bytes accessed | tf_op | source)
XLA Modules:
  0.0 558.7 jit_solution(6714454892285091216)
XLA Ops:
  6.5 0.0 all-gather.2.cloned.1.call-start
  6.5 0.7 broadcast_add_fusion
  7.3 9.0 %multiply_convert_fusion.1 = (bf16[4096,2,1,64]{0,3,2,1:T(8,128)(2,1)S(1)}, bf16[4096,2,1,64]{0,3,2,1:T(8,128)(2,1)S(1)}) fusion(s32[2,64]{1,0:T(2,128)S(1)} %broadcast_add_fusion), kind=kLoop, calls=%fused_computation.40 | loop fusion | flops 9961472 | bytes 2097664 | tf_op jit(solution)/shard_map/convert
  16.3 1.5 pad_maximum_fusion
  17.8 14.7 %fusion.25 = f32[256,4096]{1,0:T(8,128)S(1)} fusion(bf16[4096,256]{0,1:T(8,128)(2,1)} %bitcast.31, bf16[4096,4096]{1,0:T(8,128)(2,1)} %bitcast.32), kind=kOutput, calls=%fused_computation.50 | convolution fusion | flops 8589934592 | bytes 39845888 | tf_op jit(solution)/shard_map/dot_general | solution.py:64
  32.6 0.8 fusion.18
  33.4 1.7 fusion.12
  35.1 4.1 copy.7
  39.2 0.0 all-gather.2.cloned.1.call-update
  39.2 0.2 all-reduce.2.cloned.1.call-start
  39.4 229.9 %all-gather.2.cloned.1.call-done = bf16[16,2048,256]{2,1,0:T(8,128)(2,1)} async-done(((bf16[2,2048,256]{2,1,0:T(8,128)(2,1)}), bf16[16,2048,256]{2,1,0:T(8,128)(2,1)}) %all-gather.2.cloned.1.call-update) | async-done | bytes 16777232 | tf_op jit(solution)/shard_map/all_gather | solution.py:70
  269.3 8.2 %dynamic-slice_select_fusion = bf16[16,1024,256]{2,1,0:T(8,128)(2,1)} fusion(bf16[16,2048,256]{2,1,0:T(8,128)(2,1)} %all-gather.2.cloned.1.call-done, s32[]{:T(128)S(6)} %select_n.43, pred[]{:T(512)S(6)} %eq.7), kind=kLoop, calls=%fused_computation.21 | loop fusion | flops 4194304 | bytes 16777220 | tf_op jit(solution)/shard_map/jit(_where)/select_n | solution.py:13
  277.5 0.0 copy-start.2
  277.5 0.0 all-reduce.2.cloned.1.call-update
  277.6 0.6 copy-done.2
  278.2 14.1 %broadcast_multiply_fusion = bf16[16,2048,256]{2,1,0:T(8,128)(2,1)} fusion(bf16[16,2048,256]{2,1,0:T(8,128)(2,1)} %all-gather.2.cloned.1.call-done, bf16[16]{0:T(256)(128)(2,1)S(1)} %convert_element_type.33), kind=kLoop, calls=%fused_computation.22 | loop fusion | flops 8388608 | bytes 33554464 | tf_op jit(solution)/shard_map/mul | solution.py:77
  292.3 136.4 %all-reduce.2.cloned.1.call-done = bf16[16,1024,256]{2,1,0:T(8,128)(2,1)} async-done(((bf16[16,1024,256]{2,1,0:T(8,128)(2,1)}), bf16[16,1024,256]{2,1,0:T(8,128)(2,1)}) %all-reduce.2.cloned.1.call-update) | async-done | bytes 8388624 | tf_op jit(solution)/shard_map/psum | solution.py:14
  428.8 0.0 copy-start
  428.8 4.2 fusion.24
  433.0 1.6 copy-done
  434.6 7.4 %slice_negate_fusion.1 = (bf16[16,1024,64]{2,1,0:T(8,128)(2,1)}, bf16[16,1024,64]{2,1,0:T(8,128)(2,1)}, bf16[16,1024,64]{2,1,0:T(8,128)(2,1)}, bf16[16,1024,64]{2,1,0:T(8,128)(2,1)}) fusion(bf16[16,1024,256]{2,1,0:T(8,128)(2,1)S(1)} %copy-done), kind=kLoop, calls=%fused_computation.24 | loop fusion | flops 2097152 | bytes 16777216 | tf_op jit(solution)/shard_map/neg | solution.py:41
  442.0 25.1 %convolution_bitcast_fusion = f32[2048,2048]{1,0:T(8,128)} fusion(bf16[16,2048,256]{2,1,0:T(8,128)(2,1)} %broadcast_multiply_fusion, bf16[16,1024,64]{2,1,0:T(8,128)(2,1)} %get-tuple-element.12, bf16[16,1024,64]{2,1,0:T(8,128)(2,1)} %get-tuple-element.13, bf16[16,1024,128]{2,1,0:T(8,128)(2,1)S(1)} %get-tuple-element.10), kind=kOutput, calls=%fused_computation.3 | convolution fusion | flops 17205035008 | bytes 37748736 | tf_op jit(solution)/shard_map/dot_general | solution.py:51
  467.1 0.0 copy-start.1
  467.1 11.5 %slice_bitcast_fusion.1 = (f32[1,2048,1024]{2,1,0:T(8,128)}, f32[1,2048,1024]{2,1,0:T(8,128)}) fusion(f32[2048,2048]{1,0:T(8,128)} %convolution_bitcast_fusion), kind=kLoop, calls=%fused_computation.6 | loop fusion | bytes 33554432 | tf_op jit(solution)/shard_map/stack | solution.py:57
  478.5 0.0 copy-done.1
  478.5 26.3 %convolution_bitcast_fusion.1 = f32[2048,2048]{1,0:T(8,128)} fusion(bf16[16,2048,256]{2,1,0:T(8,128)(2,1)} %broadcast_multiply_fusion, bf16[16,1024,64]{2,1,0:T(8,128)(2,1)} %get-tuple-element.14, bf16[16,1024,64]{2,1,0:T(8,128)(2,1)S(1)} %copy-done.1, bf16[16,1024,128]{2,1,0:T(8,128)(2,1)S(1)} %get-tuple-element.9), kind=kOutput, calls=%fused_computation.4 | convolution fusion | flops 17205035008 | bytes 35651584 | tf_op jit(solution)/shard_map/dot_general | solution.py:51
  504.8 11.0 %slice_bitcast_fusion.3 = (f32[1,2048,1024]{2,1,0:T(8,128)}, f32[1,2048,1024]{2,1,0:T(8,128)}) fusion(f32[2048,2048]{1,0:T(8,128)} %convolution_bitcast_fusion.1), kind=kLoop, calls=%fused_computation.9 | loop fusion | bytes 33554432 | tf_op jit(solution)/shard_map/stack | solution.py:57
  515.8 17.0 %maximum_bitcast_fusion = (f32[1,2,2048,1024]{3,2,1,0:T(8,128)S(1)}, f32[1,2,2048,1024]{3,2,1,0:T(8,128)}) fusion(f32[1,2048,1024]{2,1,0:T(8,128)} %get-tuple-element.6, f32[1,2048,1024]{2,1,0:T(8,128)} %get-tuple-element.5, f32[1,2048,1024]{2,1,0:T(8,128)} %get-tuple-element.8, f32[1,2048,1024]{2,1,0:T(8,128)} %get-tuple-element.7), kind=kLoop, calls=%fused_computation.1 | loop fusion | flops 8388608 | bytes 67108864 | tf_op jit(solution)/shard_map/stack | solution.py:58
  532.8 19.0 %maximum_multiply_fusion = f32[2,2,2048,1024]{3,2,1,0:T(8,128)} fusion(f32[1,2,2048,1024]{3,2,1,0:T(8,128)} %get-tuple-element.18, f32[1,2,2048,1024]{3,2,1,0:T(8,128)S(1)} %get-tuple-element.17), kind=kLoop, calls=%fused_computation | loop fusion | flops 16777216 | bytes 67108864 | tf_op jit(solution)/shard_map/mul | solution.py:78
  (3 shorter events, 0.0 us)
Async XLA Ops:
  6.5 262.8 %all-gather.2.cloned.1.call-start = ((), (), s32[]{:S(2)}) async-start(), calls=%async_computation | async-start | bytes 18874368 | tf_op jit(solution)/shard_map/all_gather | solution.py:70
  39.2 389.6 %all-reduce.2.cloned.1.call-start = ((), (), s32[]{:S(2)}) async-start(), calls=%async_computation.1 | async-start | bytes 16777216 | tf_op jit(solution)/shard_map/psum | solution.py:14
  277.5 0.7 copy-start.2
  428.8 5.8 %copy-start = (bf16[16,1024,256]{2,1,0:T(8,128)(2,1)S(1)}, bf16[16,1024,256]{2,1,0:T(8,128)(2,1)}, u32[]{:S(2)}) copy-start(bf16[16,1024,256]{2,1,0:T(8,128)(2,1)} %all-reduce.2.cloned.1.call-done) | copy-start | bytes 25165828
  467.1 11.5 %copy-start.1 = (bf16[16,1024,64]{2,1,0:T(8,128)(2,1)S(1)}, bf16[16,1024,64]{2,1,0:T(8,128)(2,1)}, u32[]{:S(2)}) copy-start(bf16[16,1024,64]{2,1,0:T(8,128)(2,1)} %get-tuple-element.11) | copy-start | bytes 6291460
Sparse Core Ops, SparseCore 0:
  39.3 229.9 all-gather.1
  277.7 151.0 all-reduce.1
where the time goes:
time: 559 us
  waiting for transfers between devices  366 us (65%)
  other arithmetic  79.5 us (14%)
  matrix products  66.1 us (12%)
  local copies, waits for them, and re-layouts  33 us (6%)
  between operations  13.5 us (2%)
    all_gather x1, waiting for transfers between devices, shards(): row_side = lax.all_gather(whitened, 'col', axis=0, tiled=True)  230 us
    psum x1, waiting for transfers between devices, from_root(): return lax.psum(block, axis)  136 us
    dot_general x2, matrix products, pair_terms(): lax.dot_general(bin_block, prepared[band_index], (((0, 2), (0, 2)), ((),...  51.4 us
    another operation x2, local copies, waits for them, and re-layouts, pair_terms(): jnp.stack([product[:, :half_width], product[:, half_width:]], axis=0)  22.4 us
    mul x1, other arithmetic, shards(): return summed * factor  19 us
    another operation x1, other arithmetic, pair_terms(): return jnp.stack(results, axis=0)  17 us
    dot_general x1, matrix products, shards(): jnp.dot(records.reshape(seg_count * row_count, length), weights, preferre...  14.7 us
    mul x1, other arithmetic, shards(): row_side * valid_weight[:, None, None]  14.1 us
  transfers between devices with their start and end apart: 2, of which 2 were waited for; matrix products, arithmetic and copies ran while one was open for 3% of the time, Pallas kernels for 0%

commit v1 on v0

v1 whole, which is shorter than its diff:
```python
import functools
import math

import jax
import jax.numpy as jnp
from jax import lax
from jax.experimental import pallas as pl
from jax.experimental.pallas import tpu as pltpu
from jax.sharding import PartitionSpec as P


BAND = 64
NSEL = 2
LANES = 2 * BAND
FINE = 64


def fill_table(length, centre_ref, table_ref):
    lane = lax.broadcasted_iota(jnp.int32, (FINE, LANES), 1)
    step = lax.broadcasted_iota(jnp.int32, (FINE, LANES), 0)
    centre = jnp.where(lane < BAND, centre_ref[0], centre_ref[1])
    frequency = centre - BAND // 2 + jnp.where(lane < BAND, lane, lane - BAND)
    scale = 2.0 * math.pi / length
    factor = 1.0 / math.sqrt(length)
    fine = lax.rem(step * frequency, length).astype(jnp.float32) * scale
    fine_cos, fine_sin = jnp.cos(fine), jnp.sin(fine)
    for first in range(0, length // FINE, FINE):
        many = min(FINE, length // FINE - first)
        coarse = lax.rem((step + first) * frequency * FINE, length).astype(jnp.float32) * scale
        coarse_cos, coarse_sin = jnp.cos(coarse) * factor, jnp.sin(coarse) * factor
        for index in range(many):
            c = coarse_cos[index : index + 1, :]
            s = coarse_sin[index : index + 1, :]
            real = c * fine_cos - s * fine_sin
            imag = -(s * fine_cos + c * fine_sin)
            rows = pl.ds((first + index) * FINE, FINE)
            table_ref[rows, :LANES] = real.astype(jnp.bfloat16)
            table_ref[rows, LANES:] = imag.astype(jnp.bfloat16)


def front_kernel(place_ref, valid_ref, centre_ref, records_ref, out_ref, table_ref):
    segments, rows, length = records_ref.shape

    @pl.when(pl.program_id(0) == 0)
    def _():
        fill_table(length, centre_ref, table_ref)

    spectra = jnp.dot(
        records_ref[...].reshape(segments * rows, length), table_ref[...], preferred_element_type=jnp.float32
    )
    real, imag = spectra[:, :LANES], spectra[:, LANES:]
    size = jnp.sqrt(real * real + imag * imag)
    left = lax.broadcasted_iota(jnp.int32, (LANES, LANES), 0) < BAND
    top = lax.broadcasted_iota(jnp.int32, (LANES, LANES), 1) < BAND
    same = (left == top).astype(jnp.bfloat16)
    total = jnp.zeros_like(size)
    rest = size
    for _ in range(3):
        piece = rest.astype(jnp.bfloat16)
        total = total + jnp.dot(piece, same, preferred_element_type=jnp.float32)
        rest = rest - piece.astype(jnp.float32)
    inverse = 1.0 / (total * (1.0 / BAND) + 1e-06)
    lane = lax.broadcasted_iota(jnp.int32, (rows, LANES), 1) < BAND
    keep = [valid_ref[place_ref[2] * segments + s].astype(jnp.float32) for s in range(segments)]
    for part, values in ((0, real), (1, imag)):
        scaled = values * inverse
        first = scaled[:rows] * keep[0]
        second = scaled[rows:] * keep[1]
        here = pl.ds(part * LANES, LANES)
        out_ref[0, :, here] = jnp.where(lane, first, pltpu.roll(second, BAND, 1)).astype(jnp.bfloat16)
        out_ref[1, :, here] = jnp.where(lane, pltpu.roll(first, BAND, 1), second).astype(jnp.bfloat16)


def front(place, far, valid, centres, records, half_rows):
    segments, _, length = records.shape
    tile = 256
    tiles = half_rows // tile
    half = lambda s: 1 - s[0] if far else s[0]
    return pl.pallas_call(
        front_kernel,
        out_shape=jax.ShapeDtypeStruct((NSEL, half_rows, 2 * LANES), jnp.bfloat16),
        grid_spec=pltpu.PrefetchScalarGridSpec(
            num_scalar_prefetch=3,
            grid=(tiles,),
            in_specs=[pl.BlockSpec((segments, tile, length), lambda i, s, v, c: (0, half(s) * tiles + i, 0))],
            out_specs=pl.BlockSpec((NSEL, tile, 2 * LANES), lambda i, s, v, c: (0, i, 0)),
            scratch_shapes=[pltpu.VMEM((length, 2 * LANES), jnp.bfloat16)],
        ),
        cost_estimate=pl.CostEstimate(
            flops=2 * segments * half_rows * length * 256,
            bytes_accessed=2 * segments * half_rows * length,
            transcendentals=0,
        ),
    )(place, valid, centres, records)


def back_kernel(factor, units, partial, scalar_ref, *refs):
    row_refs = refs[:units]
    col_refs = [refs[units + 4 * u : units + 4 * u + 4] for u in range(units)]
    partial_ref = refs[5 * units] if partial else None
    out_ref, right_ref, arrived = refs[-3:]
    band = pl.program_id(0)

    def copies(which, at):
        return [
            pltpu.make_async_copy(col_refs[u][which].at[at], right_ref.at[at, u], arrived.at[at, u])
            for u in range(units)
        ]

    @pl.when((band == 0) & (pl.program_id(1) == 0))
    def _():
        for which in range(4):

            @pl.when(scalar_ref[1] == which)
            def _():
                for at in range(NSEL):
                    for copy in copies(which, at):
                        copy.start()

    for at in range(NSEL):

        @pl.when((band == at) & (pl.program_id(1) == 0))
        def _():
            for copy in copies(0, at):
                copy.wait()

    rows = [r[0] for r in row_refs]
    real = jnp.concatenate(rows, axis=1)
    turned = jnp.concatenate([p for r in rows for p in (r[:, LANES:], -r[:, :LANES])], axis=1)
    left = jnp.concatenate([real, turned], axis=0)
    right = jnp.concatenate([right_ref[band, u] for u in range(units)], axis=1)
    product = lax.dot_general(left, right, (((1,), (1,)), ((), ())), preferred_element_type=jnp.float32)
    many = real.shape[0]
    for part in range(2):
        value = product[part * many : (part + 1) * many] * factor
        if partial:
            value = value + partial_ref[0, part].astype(jnp.float32)
        out_ref[0, part] = value.astype(out_ref.dtype)


def back(place, far, start, count, row_units, col_units, factor, partial=None, held=None, row_count=None):
    units, col_count = len(row_units), col_units[0][0].shape[1]
    half_rows = col_count
    tile = math.gcd(count, 512)
    tiles = count // tile
    final = row_count is not None
    half = lambda s: 1 - s[0] if far else s[0]
    kept = pl.BlockSpec(memory_space=pltpu.HBM)
    in_specs = [
        pl.BlockSpec((1, tile, 2 * LANES), lambda b, i, s, first=first: (b, first // tile + i, 0))
        for _, first in row_units
    ]
    in_specs += [kept] * (4 * units)
    operands = [place, *(x for x, _ in row_units), *(c for col in col_units for c in col)]
    out_spec = pl.BlockSpec((1, 2, tile, col_count), lambda b, i, s: (b, 0, i, 0))
    if final:
        out_spec = pl.BlockSpec(
            (1, 2, tile, col_count), lambda b, i, s: (b, 0, (half(s) * half_rows + start) // tile + i, 0)
        )
    if partial is not None:
        operands.append(partial)
        begin = start // tile if final else 0
        in_specs.append(pl.BlockSpec((1, 2, tile, col_count), lambda b, i, s: (b, 0, begin + i, 0)))
    aliases = {}
    if held is not None:
        aliases = {len(operands): 0}
        operands.append(held)
        in_specs.append(kept)
    shape = (NSEL, 2, row_count if final else count, col_count)
    return pl.pallas_call(
        functools.partial(back_kernel, factor, units, partial is not None),
        out_shape=jax.ShapeDtypeStruct(shape, jnp.float32 if final else jnp.bfloat16),
        grid_spec=pltpu.PrefetchScalarGridSpec(
            num_scalar_prefetch=1,
            grid=(NSEL, tiles),
            in_specs=in_specs,
            out_specs=out_spec,
            scratch_shapes=[
                pltpu.VMEM((NSEL, units, col_count, 2 * LANES), jnp.bfloat16),
                pltpu.SemaphoreType.DMA((NSEL, units)),
            ],
        ),
        input_output_aliases=aliases,
        cost_estimate=pl.CostEstimate(
            flops=2 * NSEL * 2 * count * col_count * 256 * units,
            bytes_accessed=(4 if final else 2) * NSEL * 2 * count * col_count,
            transcendentals=0,
        ),
    )(*operands)


def ring_shards(records, centre_bins, segment_valid):
    _, row_count, _ = records.shape
    col_size = lax.axis_size("col")
    half_rows = row_count // 2
    row_index, col_index = lax.axis_index("row"), lax.axis_index("col")
    factor = 1.0 / (segment_valid.shape[0] * BAND)

    around = [(c, (c + 2) % col_size) for c in range(col_size)]
    across = [(c, c ^ 1) for c in range(col_size)]
    flat = lambda r, c: r * col_size + c
    holders = [(c // 2, c) for c in range(col_size)]
    to_y = [(flat(r, c), flat(r ^ 2, c)) for r, c in holders]
    to_core = [(flat(r, c), flat(r ^ 1, c)) for r, c in holders]
    to_far_core = [(flat(r ^ 2, c), flat(r ^ 3, c)) for r, c in holders]

    def ring(x):
        return lax.ppermute(x, "col", around)

    def cross(x):
        return lax.ppermute(x, "col", across)

    def column(x):
        over = lax.ppermute(x, ("row", "col"), to_y)
        left = lax.ppermute(x, ("row", "col"), to_core)
        right = lax.ppermute(over, ("row", "col"), to_far_core)
        return [x, left, over, right]

    apart = row_index ^ (col_index // 2)
    place = jnp.stack([col_index % 2, apart, col_index]).astype(jnp.int32)
    far = front(place, True, segment_valid, centre_bins, records, half_rows)
    near = front(place, False, segment_valid, centre_bins, records, half_rows)

    z1f = ring(far)
    x0n = cross(far)
    z1n = ring(near)
    x0f = cross(near)
    z2f = ring(z1f)
    x1n = cross(z1f)
    x1f = cross(z1n)
    z3f = ring(z2f)
    z2n = ring(z1n)
    x2n = cross(z2f)
    x2f = cross(z2n)
    z3n = ring(z2n)
    x3n = cross(z3f)
    x3f = cross(z3n)

    near_units = dict(o=near, a=x0n, b=z1n, c=x1n, d=z2n, e=x2n, g=z3n, h=x3n)
    far_units = dict(o=far, a=x0f, b=z1f, c=x1f, d=z2f, e=x2f, g=z3f, h=x3f)
    columns = {u: column(x) for u, x in near_units.items()}

    def add(name, units, partial=None, held=None, final=None):
        far_rows = name[-1] == "f"
        row_units = [((far_units if far_rows else near_units)[u], 0) for u in units]
        col_units = [columns[u] for u in units]
        return back(place, far_rows, 0, half_rows, row_units, col_units, factor, partial, held, final)

    part_n = add("pre1n", "oa")
    part_f = add("pre1f", "oa")
    part_n = add("pre2n", "bc", part_n)
    part_f = add("pre2f", "bc", part_f)
    part_n = add("pre3n", "de", part_n)
    out = add("finn", "gh", part_n, None, row_count)
    out = add("finf", "degh", part_f, out, row_count)
    return out


def gather_shards(records, centre_bins, segment_valid):
    seg_count, row_count, length = records.shape
    samples = lax.broadcasted_iota(jnp.int32, (length, 1, 1), 0)
    offsets = jnp.arange(BAND, dtype=jnp.int32) - BAND // 2
    frequencies = centre_bins[:, None] + offsets[None, :]
    angles = (samples * frequencies[None, :, :] % length).astype(jnp.float32) * (2.0 * math.pi / length)
    scale = 1.0 / math.sqrt(length)
    table = jnp.stack([jnp.cos(angles) * scale, -jnp.sin(angles) * scale], axis=2)
    table = table.reshape(length, NSEL * LANES).astype(jnp.bfloat16)
    spectra = jnp.dot(
        records.reshape(seg_count * row_count, length), table, preferred_element_type=jnp.float32
    ).reshape(seg_count * row_count, NSEL, 2, BAND)
    amplitude = jnp.mean(jnp.sqrt(spectra[:, :, 0] ** 2 + spectra[:, :, 1] ** 2), axis=2)
    whitened = (spectra / (amplitude[:, :, None, None] + 1e-06)).astype(jnp.bfloat16)
    row_side = lax.all_gather(whitened.reshape(seg_count, row_count, NSEL * LANES), "col", axis=0, tiled=True)
    row_size, col_size = lax.axis_size("row"), lax.axis_size("col")
    col_count = row_count * row_size // col_size
    column_index = lax.axis_index("col")
    start = column_index * col_count
    local = lax.dynamic_slice_in_dim(row_side, start % row_count, col_count, 1)
    local = jnp.where(lax.axis_index("row") == start // row_count, local, jnp.zeros_like(local))
    col_side = lax.psum(local, "row")
    row_side = row_side * segment_valid.astype(jnp.bfloat16)[:, None, None]
    results = []
    for band in range(NSEL):
        left = row_side[:, :, band * LANES : (band + 1) * LANES]
        right = col_side[:, :, band * LANES : (band + 1) * LANES]
        turned = jnp.concatenate([-right[:, :, BAND:], right[:, :, :BAND]], axis=2)
        for side in (right, turned):
            results.append(
                lax.dot_general(left, side, (((0, 2), (0, 2)), ((), ())), preferred_element_type=jnp.float32)
            )
    total = jnp.stack(results).reshape(NSEL, 2, row_count, col_count)
    return total * (1.0 / (segment_valid.shape[0] * BAND))


def solution(mesh):
    placed = (P("col", "row", None), P(), P())
    out = P(None, None, "row", "col")
    on_ring = mesh.shape["col"] == 2 * mesh.shape["row"] and mesh.shape["row"] == 4
    shards = ring_shards if on_ring else gather_shards
    return jax.shard_map(shards, mesh=mesh, in_specs=placed, out_specs=out, check_vma=False)
```

time: 559 us -> 268 us (0.48)
  waiting for transfers between devices: 366 us -> 79.9 us
  Pallas kernels: 0 us -> 112 us
  other arithmetic: 79.5 us -> 0.61 us
  starting transfers between devices: 0.22 us -> 72.3 us
  matrix products: 66.1 us -> 0 us
  local copies, waits for them, and re-layouts: 33 us -> 2.03 us
  between operations: 13.5 us -> 0.69 us
    all_gather x1 -> x0, waiting for transfers between devices: 230 us -> none  [shards(): row_side = lax.all_gather(whitened, 'col', axis=0, tiled=True)]
    psum x1 -> x0, waiting for transfers between devices: 136 us -> none  [from_root(): return lax.psum(block, axis)]
    pallas_call x0 -> x9, Pallas kernels: none -> 112 us  [the longest x7 87.2 us: back(): pl.pallas_call(functools.partial(back_kernel, factor, units, partial is n...]
    ppermute x0 -> x38, waiting for transfers between devices: none -> 79.9 us  [the longest x8 56.9 us: cross(): return lax.ppermute(x, 'col', across)]
    ppermute x0 -> x38, starting transfers between devices: none -> 72.3 us  [the longest x8 31.9 us: column(): over = lax.ppermute(x, ('row', 'col'), to_y)]
    dot_general x3 -> x0, matrix products: 66.1 us -> none  [the longest x2 51.4 us: pair_terms(): lax.dot_general(bin_block, prepared[band_index], (((0, 2), (0, 2)), ((),...]
    mul x2 -> x0, other arithmetic: 33.1 us -> none  [the longest x1 19 us: shards(): return summed * factor]
    another operation x3 -> x1, other arithmetic: 27.5 us -> 0.61 us  [ring_shards(): place = jnp.stack([col_index % 2, apart, col_index]).astype(jnp.int32)]
  transfers between devices with their start and end apart: 2 -> 38, of which waited for: 2 -> 11; matrix products, arithmetic and copies ran while one was open for 3% -> 0% of each run, Pallas kernels for 0% -> 31%
where the time goes in v1:
time: 268 us; the launch traced here: 267 us
  Pallas kernels  112 us (42%)
  waiting for transfers between devices  79.9 us (30%)
  starting transfers between devices  72.3 us (27%)
    pallas_call x7, Pallas kernels, back(): pl.pallas_call(functools.partial(back_kernel, factor, units, partial is n...  87.2 us
    ppermute x8, waiting for transfers between devices, cross(): return lax.ppermute(x, 'col', across)  56.9 us
    ppermute x8, starting transfers between devices, column(): over = lax.ppermute(x, ('row', 'col'), to_y)  31.9 us
    pallas_call x2, Pallas kernels, front(): pl.pallas_call(front_kernel, out_shape=jax.ShapeDtypeStruct((NSEL, half_r...  24.3 us
    ppermute x6, waiting for transfers between devices, ring(): return lax.ppermute(x, 'col', around)  23 us
    ppermute x8, starting transfers between devices, column(): left = lax.ppermute(x, ('row', 'col'), to_core)  12.6 us
    ppermute x8, starting transfers between devices, cross(): return lax.ppermute(x, 'col', across)  11.1 us
    ppermute x8, starting transfers between devices, column(): right = lax.ppermute(over, ('row', 'col'), to_far_core)  9.53 us
  transfers between devices with their start and end apart: 38, of which 11 were waited for; matrix products, arithmetic and copies ran while one was open for 0% of the time, Pallas kernels for 31%

profile of v1, /device:TPU:0, one launch (start us, length us, event | category | flops | bytes accessed | tf_op | source)
XLA Modules:
  0.0 267.0 jit_solution(18194457617047402233)
XLA Ops:
  0.0 0.6 pad_add_fusion.place_ref.scalar_ref
  0.6 12.2 %shard_map.37.refs_0_ = bf16[2,1024,256]{2,1,0:T(8,128)(2,1)} custom-call(s32[3]{0:T(128)} %pad_add_fusion.place_ref.scalar_ref, s32[16]{0:T(128)} %valid_ref.3, s32[2]{0:T(128)} %centre_ref.3, bf16[2,2048,4096]{2,1,0:T(8,128)(2,1)} %records_ref.3), custom_call_target="tpu_custom_call" | custom-call | flops 4294967296 | bytes 16777216 | tf_op jit(solution)/shard_map/pallas_call | solution.py:79
  12.8 3.0 %collective-permute-start.34 = (bf16[2,1024,256]{2,1,0:T(8,128)(2,1)}, bf16[2,1024,256]{2,1,0:T(8,128)(2,1)S(1)}, u32[]{:S(2)}, u32[]{:S(2)}) collective-permute-start(bf16[2,1024,256]{2,1,0:T(8,128)(2,1)} %shard_map.37.refs_0_), channel_id=1, source_target_pairs={{0,1},{1,0},{2,3},{3,2},{4,5},{5,4},{6,7},{7,6},{8,9},{9,8},{10,11... | collective-permute-start | bytes 3145736 | tf_op jit(solution)/shard_map/ppermute | solution.py:211
  15.8 1.6 collective-permute-start
  17.3 12.2 %shard_map.38.refs_2_.refs_0_ = bf16[2,1024,256]{2,1,0:T(8,128)(2,1)} custom-call(s32[3]{0:T(128)} %pad_add_fusion.place_ref.scalar_ref, s32[16]{0:T(128)} %valid_ref.3, s32[2]{0:T(128)} %centre_ref.3, bf16[2,2048,4096]{2,1,0:T(8,128)(2,1)} %records_ref.3), custom_call_target="tpu_custom_call" | custom-call | flops 4294967296 | bytes 16777216 | tf_op jit(solution)/shard_map/pallas_call | solution.py:79
  29.5 3.5 %collective-permute-start.32 = (bf16[2,1024,256]{2,1,0:T(8,128)(2,1)}, bf16[2,1024,256]{2,1,0:T(8,128)(2,1)S(1)}, u32[]{:S(2)}, u32[]{:S(2)}) collective-permute-start(bf16[2,1024,256]{2,1,0:T(8,128)(2,1)} %shard_map.38.refs_2_.refs_0_), channel_id=1, source_target_pairs={{0,16},{1,17},{10,26},{11,27},{20,4},{21,5},{30,14},{31,15}} | collective-permute-start | bytes 3145736 | tf_op jit(solution)/shard_map/ppermute | solution.py:214
  33.0 2.3 collective-permute-start.31
  35.3 0.5 collective-permute-start.30
  35.8 4.2 %collective-permute-done.34.refs_6_.refs_1_ = bf16[2,1024,256]{2,1,0:T(8,128)(2,1)S(1)} collective-permute-done((bf16[2,1024,256]{2,1,0:T(8,128)(2,1)}, bf16[2,1024,256]{2,1,0:T(8,128)(2,1)S(1)}, u32[]{:S(2)}, u32[]{:S(2)}) %collective-permute-start.34) | collective-permute-done | bytes 1048608 | tf_op jit(solution)/shard_map/ppermute | solution.py:211
  40.0 2.1 collective-permute-start.2
  42.1 0.4 collective-permute-done.refs_0_
  42.5 3.5 %collective-permute-start.36 = (bf16[2,1024,256]{2,1,0:T(8,128)(2,1)S(1)}, bf16[2,1024,256]{2,1,0:T(8,128)(2,1)S(1)}, u32[]{:S(2)}, u32[]{:S(2)}) collective-permute-start(bf16[2,1024,256]{2,1,0:T(8,128)(2,1)S(1)} %collective-permute-done.34.refs_6_.refs_1_), channel_id=1, source_target_pairs={{0,16},{1,17},{10,26},{11,27},{20,4},{21,5},{30,14},{31,15}} | collective-permute-start | bytes 3145736 | tf_op jit(solution)/shard_map/ppermute | solution.py:214
  46.0 1.4 collective-permute-start.35
  47.4 1.2 collective-permute-start.26
  48.5 13.9 %collective-permute-done.30.refs_1_ = bf16[2,1024,256]{2,1,0:T(8,128)(2,1)S(1)} collective-permute-done((bf16[2,1024,256]{2,1,0:T(8,128)(2,1)}, bf16[2,1024,256]{2,1,0:T(8,128)(2,1)S(1)}, u32[]{:S(2)}, u32[]{:S(2)}) %collective-permute-start.30) | collective-permute-done | bytes 1048608 | tf_op jit(solution)/shard_map/ppermute | solution.py:211
  62.4 2.1 collective-permute-start.1
  64.5 1.1 collective-permute-done.2.refs_2_.refs_0_
  65.7 0.7 collective-permute-start.33
  66.5 4.1 %collective-permute-start.24 = (bf16[2,1024,256]{2,1,0:T(8,128)(2,1)S(1)}, bf16[2,1024,256]{2,1,0:T(8,128)(2,1)S(1)}, u32[]{:S(2)}, u32[]{:S(2)}) collective-permute-start(bf16[2,1024,256]{2,1,0:T(8,128)(2,1)S(1)} %collective-permute-done.2.refs_2_.refs_0_), channel_id=1, source_target_pairs={{0,16},{1,17},{10,26},{11,27},{20,4},{21,5},{30,14},{31,15}} | collective-permute-start | bytes 3145736 | tf_op jit(solution)/shard_map/ppermute | solution.py:214
  70.6 0.0 collective-permute-done.35.refs_7_
  70.6 1.4 collective-permute-start.23
  72.0 12.1 %collective-permute-done.26.refs_6_.refs_1_ = bf16[2,1024,256]{2,1,0:T(8,128)(2,1)S(1)} collective-permute-done((bf16[2,1024,256]{2,1,0:T(8,128)(2,1)S(1)}, bf16[2,1024,256]{2,1,0:T(8,128)(2,1)S(1)}, u32[]{:S(2)}, u32[]{:S(2)}) %collective-permute-start.26) | collective-permute-done | bytes 1048608 | tf_op jit(solution)/shard_map/ppermute | solution.py:211
  84.1 1.7 collective-permute-start.22
  85.8 2.1 collective-permute-done.1.refs_0_
  88.0 0.0 collective-permute-start.3
  88.0 0.0 collective-permute-done.33.refs_5_
  88.0 0.7 collective-permute-start.37
  88.7 0.0 collective-permute-done.24.refs_4_
  88.7 4.1 %collective-permute-start.28 = (bf16[2,1024,256]{2,1,0:T(8,128)(2,1)S(1)}, bf16[2,1024,256]{2,1,0:T(8,128)(2,1)S(1)}, u32[]{:S(2)}, u32[]{:S(2)}) collective-permute-start(bf16[2,1024,256]{2,1,0:T(8,128)(2,1)S(1)} %collective-permute-done.26.refs_6_.refs_1_), channel_id=1, source_target_pairs={{0,16},{1,17},{10,26},{11,27},{20,4},{21,5},{30,14},{31,15}} | collective-permute-start | bytes 3145736 | tf_op jit(solution)/shard_map/ppermute | solution.py:214
  92.9 1.4 collective-permute-start.27
  94.3 14.1 %collective-permute-done.22.refs_1_ = bf16[2,1024,256]{2,1,0:T(8,128)(2,1)S(1)} collective-permute-done((bf16[2,1024,256]{2,1,0:T(8,128)(2,1)S(1)}, bf16[2,1024,256]{2,1,0:T(8,128)(2,1)S(1)}, u32[]{:S(2)}, u32[]{:S(2)}) %collective-permute-start.22) | collective-permute-done | bytes 1048608 | tf_op jit(solution)/shard_map/ppermute | solution.py:211
  108.4 1.5 collective-permute-start.11
  109.8 2.5 collective-permute-done.3.refs_0_.refs_2_.refs_4_
  112.3 0.7 collective-permute-start.25
  113.1 0.0 collective-permute-done.28.refs_8_
  113.1 4.8 %collective-permute-start.9 = (bf16[2,1024,256]{2,1,0:T(8,128)(2,1)S(1)}, bf16[2,1024,256]{2,1,0:T(8,128)(2,1)}, u32[]{:S(2)}, u32[]{:S(2)}) collective-permute-start(bf16[2,1024,256]{2,1,0:T(8,128)(2,1)S(1)} %collective-permute-done.3.refs_0_.refs_2_.refs_4_), channel_id=1, source_target_pairs={{0,16},{1,17},{10,26},{11,27},{20,4},{21,5},{30,14},{31,15}} | collective-permute-start | bytes 3145736 | tf_op jit(solution)/shard_map/ppermute | solution.py:214
  117.9 1.4 collective-permute-start.8
  119.3 12.6 %collective-permute-done.11.refs_1_.refs_6_.refs_8_ = bf16[2,1024,256]{2,1,0:T(8,128)(2,1)S(1)} collective-permute-done((bf16[2,1024,256]{2,1,0:T(8,128)(2,1)S(1)}, bf16[2,1024,256]{2,1,0:T(8,128)(2,1)S(1)}, u32[]{:S(2)}, u32[]{:S(2)}) %collective-permute-start.11) | collective-permute-done | bytes 1048608 | tf_op jit(solution)/shard_map/ppermute | solution.py:211
  131.9 1.3 collective-permute-start.6
  133.1 4.7 %collective-permute-done.5.refs_2_ = bf16[2,1024,256]{2,1,0:T(8,128)(2,1)S(1)} collective-permute-done((bf16[2,1024,256]{2,1,0:T(8,128)(2,1)S(1)}, bf16[2,1024,256]{2,1,0:T(8,128)(2,1)S(1)}, u32[]{:S(2)}, u32[]{:S(2)}) %collective-permute-start.5) | collective-permute-done | bytes 1048608 | tf_op jit(solution)/shard_map/ppermute | solution.py:208
  137.8 0.7 collective-permute-start.29
  138.5 1.2 collective-permute-start.18
  139.7 5.0 %collective-permute-start.13 = (bf16[2,1024,256]{2,1,0:T(8,128)(2,1)S(1)}, bf16[2,1024,256]{2,1,0:T(8,128)(2,1)}, u32[]{:S(2)}, u32[]{:S(2)}) collective-permute-start(bf16[2,1024,256]{2,1,0:T(8,128)(2,1)S(1)} %collective-permute-done.11.refs_1_.refs_6_.refs_8_), channel_id=1, source_target_pairs={{0,16},{1,17},{10,26},{11,27},{20,4},{21,5},{30,14},{31,15}} | collective-permute-start | bytes 3145736 | tf_op jit(solution)/shard_map/ppermute | solution.py:214
  144.7 1.3 collective-permute-start.12
  146.1 12.2 %collective-permute-done.6.refs_0_.refs_2_.refs_12_ = bf16[2,1024,256]{2,1,0:T(8,128)(2,1)S(1)} collective-permute-done((bf16[2,1024,256]{2,1,0:T(8,128)(2,1)S(1)}, bf16[2,1024,256]{2,1,0:T(8,128)(2,1)S(1)}, u32[]{:S(2)}, u32[]{:S(2)}) %collective-permute-start.6) | collective-permute-done | bytes 1048608 | tf_op jit(solution)/shard_map/ppermute | solution.py:208
  158.3 1.7 collective-permute-start.10
  159.9 4.6 %collective-permute-start.16 = (bf16[2,1024,256]{2,1,0:T(8,128)(2,1)S(1)}, bf16[2,1024,256]{2,1,0:T(8,128)(2,1)}, u32[]{:S(2)}, u32[]{:S(2)}) collective-permute-start(bf16[2,1024,256]{2,1,0:T(8,128)(2,1)S(1)} %collective-permute-done.6.refs_0_.refs_2_.refs_12_), channel_id=1, source_target_pairs={{0,16},{1,17},{10,26},{11,27},{20,4},{21,5},{30,14},{31,15}} | collective-permute-start | bytes 3145736 | tf_op jit(solution)/shard_map/ppermute | solution.py:214
  164.5 2.3 collective-permute-start.20
  166.8 2.2 collective-permute-start.15
  169.1 1.0 copy-done.7
  170.1 1.6 collective-permute-start.14
  171.8 9.8 %shard_map.41.refs_10_ = bf16[2,2,1024,1024]{3,2,1,0:T(8,128)(2,1)} custom-call(s32[3]{0:T(128)} %pad_add_fusion.place_ref.scalar_ref, bf16[2,1024,256]{2,1,0:T(8,128)(2,1)} %shard_map.38.refs_2_.refs_0_, bf16[2,1024,256]{2,1,0:T(8,128)(2,1)} %copy-done.5, bf16[2,1024,256]{2,1,0:T(8,128)(2,1)} %shard_map.38.refs_2_.refs_0_, ...), custom_call_target="tpu_custom_call" | custom-call | flops 4294967296 | bytes 8388608 | tf_op jit(solution)/shard_map/pallas_call | solution.py:170
  181.6 9.7 %shard_map.39.refs_10_ = bf16[2,2,1024,1024]{3,2,1,0:T(8,128)(2,1)} custom-call(s32[3]{0:T(128)} %pad_add_fusion.place_ref.scalar_ref, bf16[2,1024,256]{2,1,0:T(8,128)(2,1)} %shard_map.37.refs_0_, bf16[2,1024,256]{2,1,0:T(8,128)(2,1)} %copy-done.24, bf16[2,1024,256]{2,1,0:T(8,128)(2,1)} %shard_map.38.refs_2_.refs_0_, ...), custom_call_target="tpu_custom_call" | custom-call | flops 4294967296 | bytes 8388608 | tf_op jit(solution)/shard_map/pallas_call | solution.py:170
  191.3 1.4 collective-permute-start.19
  192.7 1.7 collective-permute-start.17
  194.4 1.6 collective-permute-start.21
  196.0 12.1 %shard_map.42.refs_10_ = bf16[2,2,1024,1024]{3,2,1,0:T(8,128)(2,1)} custom-call(s32[3]{0:T(128)} %pad_add_fusion.place_ref.scalar_ref, bf16[2,1024,256]{2,1,0:T(8,128)(2,1)} %copy-done.3, bf16[2,1024,256]{2,1,0:T(8,128)(2,1)} %copy-done.4, bf16[2,1024,256]{2,1,0:T(8,128)(2,1)} %copy-done.3, bf16[2,1024,256]{2,1,0:T(8,128)(2,1)} %copy-done.10, ...), custom_call_target="tpu_custom_call" | custom-call | flops 4294967296 | bytes 8388608 | tf_op jit(solution)/shard_map/pallas_call | solution.py:170
  208.1 1.6 collective-permute-start.4
  209.8 0.5 collective-permute-start.7
  210.2 12.2 %shard_map.40.refs_20_ = bf16[2,2,1024,1024]{3,2,1,0:T(8,128)(2,1)} custom-call(s32[3]{0:T(128)} %pad_add_fusion.place_ref.scalar_ref, bf16[2,1024,256]{2,1,0:T(8,128)(2,1)} %copy-done.22, bf16[2,1024,256]{2,1,0:T(8,128)(2,1)} %copy-done.23, bf16[2,1024,256]{2,1,0:T(8,128)(2,1)} %copy-done.3, bf16[2,1024,256]{2,1,0:T(8,128)(2,1)} %copy-done.10, ...), custom_call_target="tpu_custom_call" | custom-call | flops 4294967296 | bytes 8388608 | tf_op jit(solution)/shard_map/pallas_call | solution.py:170
  222.5 12.2 %shard_map.43.refs_10_ = bf16[2,2,1024,1024]{3,2,1,0:T(8,128)(2,1)} custom-call(s32[3]{0:T(128)} %pad_add_fusion.place_ref.scalar_ref, bf16[2,1024,256]{2,1,0:T(8,128)(2,1)} %copy-done, bf16[2,1024,256]{2,1,0:T(8,128)(2,1)} %copy-done.1, bf16[2,1024,256]{2,1,0:T(8,128)(2,1)} %copy-done, bf16[2,1024,256]{2,1,0:T(8,128)(2,1)} %copy-done.6, ...), custom_call_target="tpu_custom_call" | custom-call | flops 4294967296 | bytes 8388608 | tf_op jit(solution)/shard_map/pallas_call | solution.py:170
  234.7 0.9 copy-done.8
  235.7 13.9 %shard_map.44.refs_21_ = f32[2,2,2048,1024]{3,2,1,0:T(8,128)} custom-call(s32[3]{0:T(128)} %pad_add_fusion.place_ref.scalar_ref, bf16[2,1024,256]{2,1,0:T(8,128)(2,1)} %copy-done.2, bf16[2,1024,256]{2,1,0:T(8,128)(2,1)} %collective-permute-done.18.refs_1_.refs_6_.refs_16_, bf16[2,1024,256]{2,1,0:T(8,128)(2,1)} %copy-done.2, ...), custom_call_target="tpu_custom_call" | custom-call | flops 4294967296 | bytes 16777216 | tf_op jit(solution)/shard_map/pallas_call | solution.py:170
  249.6 17.2 %shard_map.45 = f32[2,2,2048,1024]{3,2,1,0:T(8,128)} custom-call(s32[3]{0:T(128)} %pad_add_fusion.place_ref.scalar_ref, bf16[2,1024,256]{2,1,0:T(8,128)(2,1)} %copy-done.20, bf16[2,1024,256]{2,1,0:T(8,128)(2,1)} %collective-permute-done.4.refs_1_, bf16[2,1024,256]{2,1,0:T(8,128)(2,1)} %copy-done.21, ...), custom_call_target="tpu_custom_call", output_to_operand_aliasing={{}: (22, {})} | custom-call | flops 8589934592 | bytes 16777216 | tf_op jit(solution)/shard_map/pallas_call | solution.py:170
  (72 shorter events, 0.2 us)
Async XLA Ops:
  12.8 27.2 %collective-permute-start.34 = (bf16[2,1024,256]{2,1,0:T(8,128)(2,1)}, bf16[2,1024,256]{2,1,0:T(8,128)(2,1)S(1)}, u32[]{:S(2)}, u32[]{:S(2)}) collective-permute-start(bf16[2,1024,256]{2,1,0:T(8,128)(2,1)} %shard_map.37.refs_0_), channel_id=1, source_target_pairs={{0,1},{1,0},{2,3},{3,2},{4,5},{5,4},{6,7},{7,6},{8,9},{9,8},{10,11... | collective-permute-start | bytes 3145736 | tf_op jit(solution)/shard_map/ppermute | solution.py:211
  15.8 26.7 %collective-permute-start = (bf16[2,1024,256]{2,1,0:T(8,128)(2,1)}, bf16[2,1024,256]{2,1,0:T(8,128)(2,1)S(1)}, u32[]{:S(2)}, u32[]{:S(2)}) collective-permute-start(bf16[2,1024,256]{2,1,0:T(8,128)(2,1)} %shard_map.37.refs_0_), channel_id=1, source_target_pairs={{0,2},{1,3},{2,4},{3,5},{4,6},{5,7},{6,0},{7,1},{8,10},{9,11},{10,... | collective-permute-start | bytes 3145736 | tf_op jit(solution)/shard_map/ppermute | solution.py:208
  29.5 16.5 %collective-permute-start.32 = (bf16[2,1024,256]{2,1,0:T(8,128)(2,1)}, bf16[2,1024,256]{2,1,0:T(8,128)(2,1)S(1)}, u32[]{:S(2)}, u32[]{:S(2)}) collective-permute-start(bf16[2,1024,256]{2,1,0:T(8,128)(2,1)} %shard_map.38.refs_2_.refs_0_), channel_id=1, source_target_pairs={{0,16},{1,17},{10,26},{11,27},{20,4},{21,5},{30,14},{31,15}} | collective-permute-start | bytes 3145736 | tf_op jit(solution)/shard_map/ppermute | solution.py:214
  33.0 14.4 %collective-permute-start.31 = (bf16[2,1024,256]{2,1,0:T(8,128)(2,1)}, bf16[2,1024,256]{2,1,0:T(8,128)(2,1)}, u32[]{:S(2)}, u32[]{:S(2)}) collective-permute-start(bf16[2,1024,256]{2,1,0:T(8,128)(2,1)} %shard_map.38.refs_2_.refs_0_), channel_id=1, source_target_pairs={{0,8},{1,9},{10,2},{11,3},{20,28},{21,29},{30,22},{31,23}} | collective-permute-start | bytes 3145736 | tf_op jit(solution)/shard_map/ppermute | solution.py:215
  35.3 27.2 %collective-permute-start.30 = (bf16[2,1024,256]{2,1,0:T(8,128)(2,1)}, bf16[2,1024,256]{2,1,0:T(8,128)(2,1)S(1)}, u32[]{:S(2)}, u32[]{:S(2)}) collective-permute-start(bf16[2,1024,256]{2,1,0:T(8,128)(2,1)} %shard_map.38.refs_2_.refs_0_), channel_id=1, source_target_pairs={{0,1},{1,0},{2,3},{3,2},{4,5},{5,4},{6,7},{7,6},{8,9},{9,8},{10,11... | collective-permute-start | bytes 3145736 | tf_op jit(solution)/shard_map/ppermute | solution.py:211
  40.0 45.8 %copy-start.5 = (bf16[2,1024,256]{2,1,0:T(8,128)(2,1)}, bf16[2,1024,256]{2,1,0:T(8,128)(2,1)S(1)}, u32[]{:S(2)}) copy-start(bf16[2,1024,256]{2,1,0:T(8,128)(2,1)S(1)} %collective-permute-done.34.refs_6_.refs_1_) | copy-start | bytes 3145732
  40.0 25.7 %collective-permute-start.2 = (bf16[2,1024,256]{2,1,0:T(8,128)(2,1)}, bf16[2,1024,256]{2,1,0:T(8,128)(2,1)S(1)}, u32[]{:S(2)}, u32[]{:S(2)}) collective-permute-start(bf16[2,1024,256]{2,1,0:T(8,128)(2,1)} %shard_map.38.refs_2_.refs_0_), channel_id=1, source_target_pairs={{0,2},{1,3},{2,4},{3,5},{4,6},{5,7},{6,0},{7,1},{8,10},{9,11},{10,... | collective-permute-start | bytes 3145736 | tf_op jit(solution)/shard_map/ppermute | solution.py:208
  42.5 51.8 %copy-start.22 = (bf16[2,1024,256]{2,1,0:T(8,128)(2,1)}, bf16[2,1024,256]{2,1,0:T(8,128)(2,1)S(1)}, u32[]{:S(2)}) copy-start(bf16[2,1024,256]{2,1,0:T(8,128)(2,1)S(1)} %collective-permute-done.refs_0_) | copy-start | bytes 3145732
  42.5 24.0 %collective-permute-start.36 = (bf16[2,1024,256]{2,1,0:T(8,128)(2,1)S(1)}, bf16[2,1024,256]{2,1,0:T(8,128)(2,1)S(1)}, u32[]{:S(2)}, u32[]{:S(2)}) collective-permute-start(bf16[2,1024,256]{2,1,0:T(8,128)(2,1)S(1)} %collective-permute-done.34.refs_6_.refs_1_), channel_id=1, source_target_pairs={{0,16},{1,17},{10,26},{11,27},{20,4},{21,5},{30,14},{31,15}} | collective-permute-start | bytes 3145736 | tf_op jit(solution)/shard_map/ppermute | solution.py:214
  46.0 42.7 %copy-start.15 = (bf16[2,1024,256]{2,1,0:T(8,128)(2,1)}, bf16[2,1024,256]{2,1,0:T(8,128)(2,1)S(1)}, u32[]{:S(2)}) copy-start(bf16[2,1024,256]{2,1,0:T(8,128)(2,1)S(1)} %collective-permute-done.32.refs_4_) | copy-start | bytes 3145732
  46.0 24.6 %collective-permute-start.35 = (bf16[2,1024,256]{2,1,0:T(8,128)(2,1)S(1)}, bf16[2,1024,256]{2,1,0:T(8,128)(2,1)S(1)}, u32[]{:S(2)}, u32[]{:S(2)}) collective-permute-start(bf16[2,1024,256]{2,1,0:T(8,128)(2,1)S(1)} %collective-permute-done.34.refs_6_.refs_1_), channel_id=1, source_target_pairs={{0,8},{1,9},{10,2},{11,3},{20,28},{21,29},{30,22},{31,23}} | collective-permute-start | bytes 3145736 | tf_op jit(solution)/shard_map/ppermute | solution.py:215
  47.4 36.7 %collective-permute-start.26 = (bf16[2,1024,256]{2,1,0:T(8,128)(2,1)S(1)}, bf16[2,1024,256]{2,1,0:T(8,128)(2,1)S(1)}, u32[]{:S(2)}, u32[]{:S(2)}) collective-permute-start(bf16[2,1024,256]{2,1,0:T(8,128)(2,1)S(1)} %collective-permute-done.refs_0_), channel_id=1, source_target_pairs={{0,1},{1,0},{2,3},{3,2},{4,5},{5,4},{6,7},{7,6},{8,9},{9,8},{10,11... | collective-permute-start | bytes 3145736 | tf_op jit(solution)/shard_map/ppermute | solution.py:211
  62.4 4.0 %copy-start.24 = (bf16[2,1024,256]{2,1,0:T(8,128)(2,1)}, bf16[2,1024,256]{2,1,0:T(8,128)(2,1)S(1)}, u32[]{:S(2)}) copy-start(bf16[2,1024,256]{2,1,0:T(8,128)(2,1)S(1)} %collective-permute-done.30.refs_1_) | copy-start | bytes 3145732
  62.4 25.5 %collective-permute-start.1 = (bf16[2,1024,256]{2,1,0:T(8,128)(2,1)S(1)}, bf16[2,1024,256]{2,1,0:T(8,128)(2,1)S(1)}, u32[]{:S(2)}, u32[]{:S(2)}) collective-permute-start(bf16[2,1024,256]{2,1,0:T(8,128)(2,1)S(1)} %collective-permute-done.refs_0_), channel_id=1, source_target_pairs={{0,2},{1,3},{2,4},{3,5},{4,6},{5,7},{6,0},{7,1},{8,10},{9,11},{10,... | collective-permute-start | bytes 3145736 | tf_op jit(solution)/shard_map/ppermute | solution.py:208
  65.7 103.4 %copy-start.3 = (bf16[2,1024,256]{2,1,0:T(8,128)(2,1)}, bf16[2,1024,256]{2,1,0:T(8,128)(2,1)S(1)}, u32[]{:S(2)}) copy-start(bf16[2,1024,256]{2,1,0:T(8,128)(2,1)S(1)} %collective-permute-done.2.refs_2_.refs_0_) | copy-start | bytes 3145732
  65.7 22.3 %collective-permute-start.33 = (bf16[2,1024,256]{2,1,0:T(8,128)(2,1)S(1)}, bf16[2,1024,256]{2,1,0:T(8,128)(2,1)S(1)}, u32[]{:S(2)}, u32[]{:S(2)}) collective-permute-start(bf16[2,1024,256]{2,1,0:T(8,128)(2,1)S(1)} %collective-permute-done.32.refs_4_), channel_id=1, source_target_pairs={{16,24},{17,25},{26,18},{27,19},{4,12},{5,13},{14,6},{15,7}} | collective-permute-start | bytes 3145736 | tf_op jit(solution)/shard_map/ppermute | solution.py:216
  66.4 45.9 %copy-start.16 = (bf16[2,1024,256]{2,1,0:T(8,128)(2,1)}, bf16[2,1024,256]{2,1,0:T(8,128)(2,1)S(1)}, u32[]{:S(2)}) copy-start(bf16[2,1024,256]{2,1,0:T(8,128)(2,1)S(1)} %collective-permute-done.36.refs_8_) | copy-start | bytes 3145732
  66.5 22.3 %collective-permute-start.24 = (bf16[2,1024,256]{2,1,0:T(8,128)(2,1)S(1)}, bf16[2,1024,256]{2,1,0:T(8,128)(2,1)S(1)}, u32[]{:S(2)}, u32[]{:S(2)}) collective-permute-start(bf16[2,1024,256]{2,1,0:T(8,128)(2,1)S(1)} %collective-permute-done.2.refs_2_.refs_0_), channel_id=1, source_target_pairs={{0,16},{1,17},{10,26},{11,27},{20,4},{21,5},{30,14},{31,15}} | collective-permute-start | bytes 3145736 | tf_op jit(solution)/shard_map/ppermute | solution.py:214
  70.6 22.3 %copy-start.17 = (bf16[2,1024,256]{2,1,0:T(8,128)(2,1)}, bf16[2,1024,256]{2,1,0:T(8,128)(2,1)S(1)}, u32[]{:S(2)}) copy-start(bf16[2,1024,256]{2,1,0:T(8,128)(2,1)S(1)} %collective-permute-done.35.refs_7_) | copy-start | bytes 3145732
  70.6 22.3 %collective-permute-start.23 = (bf16[2,1024,256]{2,1,0:T(8,128)(2,1)S(1)}, bf16[2,1024,256]{2,1,0:T(8,128)(2,1)S(1)}, u32[]{:S(2)}, u32[]{:S(2)}) collective-permute-start(bf16[2,1024,256]{2,1,0:T(8,128)(2,1)S(1)} %collective-permute-done.2.refs_2_.refs_0_), channel_id=1, source_target_pairs={{0,8},{1,9},{10,2},{11,3},{20,28},{21,29},{30,22},{31,23}} | collective-permute-start | bytes 3145736 | tf_op jit(solution)/shard_map/ppermute | solution.py:215
  84.1 85.0 %copy-start.4 = (bf16[2,1024,256]{2,1,0:T(8,128)(2,1)}, bf16[2,1024,256]{2,1,0:T(8,128)(2,1)S(1)}, u32[]{:S(2)}) copy-start(bf16[2,1024,256]{2,1,0:T(8,128)(2,1)S(1)} %collective-permute-done.26.refs_6_.refs_1_) | copy-start | bytes 3145732
  84.1 24.3 %collective-permute-start.22 = (bf16[2,1024,256]{2,1,0:T(8,128)(2,1)S(1)}, bf16[2,1024,256]{2,1,0:T(8,128)(2,1)S(1)}, u32[]{:S(2)}, u32[]{:S(2)}) collective-permute-start(bf16[2,1024,256]{2,1,0:T(8,128)(2,1)S(1)} %collective-permute-done.2.refs_2_.refs_0_), channel_id=1, source_target_pairs={{0,1},{1,0},{2,3},{3,2},{4,5},{5,4},{6,7},{7,6},{8,9},{9,8},{10,11... | collective-permute-start | bytes 3145736 | tf_op jit(solution)/shard_map/ppermute | solution.py:211
  88.0 81.1 %copy-start.20 = (bf16[2,1024,256]{2,1,0:T(8,128)(2,1)}, bf16[2,1024,256]{2,1,0:T(8,128)(2,1)S(1)}, u32[]{:S(2)}) copy-start(bf16[2,1024,256]{2,1,0:T(8,128)(2,1)S(1)} %collective-permute-done.1.refs_0_) | copy-start | bytes 3145732
  88.0 24.3 %collective-permute-start.3 = (bf16[2,1024,256]{2,1,0:T(8,128)(2,1)S(1)}, bf16[2,1024,256]{2,1,0:T(8,128)(2,1)S(1)}, u32[]{:S(2)}, u32[]{:S(2)}) collective-permute-start(bf16[2,1024,256]{2,1,0:T(8,128)(2,1)S(1)} %collective-permute-done.2.refs_2_.refs_0_), channel_id=1, source_target_pairs={{0,2},{1,3},{2,4},{3,5},{4,6},{5,7},{6,0},{7,1},{8,10},{9,11},{10,... | collective-permute-start | bytes 3145736 | tf_op jit(solution)/shard_map/ppermute | solution.py:208
  88.0 29.9 %copy-start.18 = (bf16[2,1024,256]{2,1,0:T(8,128)(2,1)}, bf16[2,1024,256]{2,1,0:T(8,128)(2,1)S(1)}, u32[]{:S(2)}) copy-start(bf16[2,1024,256]{2,1,0:T(8,128)(2,1)S(1)} %collective-permute-done.33.refs_5_) | copy-start | bytes 3145732
  88.0 24.3 %collective-permute-start.37 = (bf16[2,1024,256]{2,1,0:T(8,128)(2,1)S(1)}, bf16[2,1024,256]{2,1,0:T(8,128)(2,1)S(1)}, u32[]{:S(2)}, u32[]{:S(2)}) collective-permute-start(bf16[2,1024,256]{2,1,0:T(8,128)(2,1)S(1)} %collective-permute-done.36.refs_8_), channel_id=1, source_target_pairs={{16,24},{17,25},{26,18},{27,19},{4,12},{5,13},{14,6},{15,7}} | collective-permute-start | bytes 3145736 | tf_op jit(solution)/shard_map/ppermute | solution.py:216
  88.7 56.0 %copy-start.9 = (bf16[2,1024,256]{2,1,0:T(8,128)(2,1)}, bf16[2,1024,256]{2,1,0:T(8,128)(2,1)S(1)}, u32[]{:S(2)}) copy-start(bf16[2,1024,256]{2,1,0:T(8,128)(2,1)S(1)} %collective-permute-done.24.refs_4_) | copy-start | bytes 3145732
  88.7 24.3 %collective-permute-start.28 = (bf16[2,1024,256]{2,1,0:T(8,128)(2,1)S(1)}, bf16[2,1024,256]{2,1,0:T(8,128)(2,1)S(1)}, u32[]{:S(2)}, u32[]{:S(2)}) collective-permute-start(bf16[2,1024,256]{2,1,0:T(8,128)(2,1)S(1)} %collective-permute-done.26.refs_6_.refs_1_), channel_id=1, source_target_pairs={{0,16},{1,17},{10,26},{11,27},{20,4},{21,5},{30,14},{31,15}} | collective-permute-start | bytes 3145736 | tf_op jit(solution)/shard_map/ppermute | solution.py:214
  92.9 25.0 %copy-start.10 = (bf16[2,1024,256]{2,1,0:T(8,128)(2,1)}, bf16[2,1024,256]{2,1,0:T(8,128)(2,1)S(1)}, u32[]{:S(2)}) copy-start(bf16[2,1024,256]{2,1,0:T(8,128)(2,1)S(1)} %collective-permute-done.23.refs_3_) | copy-start | bytes 3145732
  92.9 25.0 %collective-permute-start.27 = (bf16[2,1024,256]{2,1,0:T(8,128)(2,1)S(1)}, bf16[2,1024,256]{2,1,0:T(8,128)(2,1)S(1)}, u32[]{:S(2)}, u32[]{:S(2)}) collective-permute-start(bf16[2,1024,256]{2,1,0:T(8,128)(2,1)S(1)} %collective-permute-done.26.refs_6_.refs_1_), channel_id=1, source_target_pairs={{0,8},{1,9},{10,2},{11,3},{20,28},{21,29},{30,22},{31,23}} | collective-permute-start | bytes 3145736 | tf_op jit(solution)/shard_map/ppermute | solution.py:215
  108.4 1.5 copy-start.23
  108.4 23.5 %collective-permute-start.11 = (bf16[2,1024,256]{2,1,0:T(8,128)(2,1)S(1)}, bf16[2,1024,256]{2,1,0:T(8,128)(2,1)S(1)}, u32[]{:S(2)}, u32[]{:S(2)}) collective-permute-start(bf16[2,1024,256]{2,1,0:T(8,128)(2,1)S(1)} %collective-permute-done.1.refs_0_), channel_id=1, source_target_pairs={{0,1},{1,0},{2,3},{3,2},{4,5},{5,4},{6,7},{7,6},{8,9},{9,8},{10,11... | collective-permute-start | bytes 3145736 | tf_op jit(solution)/shard_map/ppermute | solution.py:211
  112.3 95.8 %copy-start = (bf16[2,1024,256]{2,1,0:T(8,128)(2,1)}, bf16[2,1024,256]{2,1,0:T(8,128)(2,1)S(1)}, u32[]{:S(2)}) copy-start(bf16[2,1024,256]{2,1,0:T(8,128)(2,1)S(1)} %collective-permute-done.3.refs_0_.refs_2_.refs_4_) | copy-start | bytes 3145732
  112.3 25.5 %collective-permute-start.5 = (bf16[2,1024,256]{2,1,0:T(8,128)(2,1)S(1)}, bf16[2,1024,256]{2,1,0:T(8,128)(2,1)S(1)}, u32[]{:S(2)}, u32[]{:S(2)}) collective-permute-start(bf16[2,1024,256]{2,1,0:T(8,128)(2,1)S(1)} %collective-permute-done.1.refs_0_), channel_id=1, source_target_pairs={{0,2},{1,3},{2,4},{3,5},{4,6},{5,7},{6,0},{7,1},{8,10},{9,11},{10,... | collective-permute-start | bytes 3145736 | tf_op jit(solution)/shard_map/ppermute | solution.py:208
  112.3 20.8 %copy-start.19 = (bf16[2,1024,256]{2,1,0:T(8,128)(2,1)}, bf16[2,1024,256]{2,1,0:T(8,128)(2,1)S(1)}, u32[]{:S(2)}) copy-start(bf16[2,1024,256]{2,1,0:T(8,128)(2,1)S(1)} %collective-permute-done.37.refs_9_) | copy-start | bytes 3145732
  112.3 26.2 %collective-permute-start.25 = (bf16[2,1024,256]{2,1,0:T(8,128)(2,1)S(1)}, bf16[2,1024,256]{2,1,0:T(8,128)(2,1)S(1)}, u32[]{:S(2)}, u32[]{:S(2)}) collective-permute-start(bf16[2,1024,256]{2,1,0:T(8,128)(2,1)S(1)} %collective-permute-done.24.refs_4_), channel_id=1, source_target_pairs={{16,24},{17,25},{26,18},{27,19},{4,12},{5,13},{14,6},{15,7}} | collective-permute-start | bytes 3145736 | tf_op jit(solution)/shard_map/ppermute | solution.py:216
  113.1 56.0 %copy-start.11 = (bf16[2,1024,256]{2,1,0:T(8,128)(2,1)}, bf16[2,1024,256]{2,1,0:T(8,128)(2,1)S(1)}, u32[]{:S(2)}) copy-start(bf16[2,1024,256]{2,1,0:T(8,128)(2,1)S(1)} %collective-permute-done.28.refs_8_) | copy-start | bytes 3145732
  113.1 26.6 %collective-permute-start.9 = (bf16[2,1024,256]{2,1,0:T(8,128)(2,1)S(1)}, bf16[2,1024,256]{2,1,0:T(8,128)(2,1)}, u32[]{:S(2)}, u32[]{:S(2)}) collective-permute-start(bf16[2,1024,256]{2,1,0:T(8,128)(2,1)S(1)} %collective-permute-done.3.refs_0_.refs_2_.refs_4_), channel_id=1, source_target_pairs={{0,16},{1,17},{10,26},{11,27},{20,4},{21,5},{30,14},{31,15}} | collective-permute-start | bytes 3145736 | tf_op jit(solution)/shard_map/ppermute | solution.py:214
  117.9 51.2 %copy-start.12 = (bf16[2,1024,256]{2,1,0:T(8,128)(2,1)}, bf16[2,1024,256]{2,1,0:T(8,128)(2,1)S(1)}, u32[]{:S(2)}) copy-start(bf16[2,1024,256]{2,1,0:T(8,128)(2,1)S(1)} %collective-permute-done.27.refs_7_) | copy-start | bytes 3145732
  117.9 26.8 %collective-permute-start.8 = (bf16[2,1024,256]{2,1,0:T(8,128)(2,1)S(1)}, bf16[2,1024,256]{2,1,0:T(8,128)(2,1)S(1)}, u32[]{:S(2)}, u32[]{:S(2)}) collective-permute-start(bf16[2,1024,256]{2,1,0:T(8,128)(2,1)S(1)} %collective-permute-done.3.refs_0_.refs_2_.refs_4_), channel_id=1, source_target_pairs={{0,8},{1,9},{10,2},{11,3},{20,28},{21,29},{30,22},{31,23}} | collective-permute-start | bytes 3145736 | tf_op jit(solution)/shard_map/ppermute | solution.py:215
  131.9 49.7 %copy-start.1 = (bf16[2,1024,256]{2,1,0:T(8,128)(2,1)}, bf16[2,1024,256]{2,1,0:T(8,128)(2,1)S(1)}, u32[]{:S(2)}) copy-start(bf16[2,1024,256]{2,1,0:T(8,128)(2,1)S(1)} %collective-permute-done.11.refs_1_.refs_6_.refs_8_) | copy-start | bytes 3145732
  131.9 26.4 %collective-permute-start.6 = (bf16[2,1024,256]{2,1,0:T(8,128)(2,1)S(1)}, bf16[2,1024,256]{2,1,0:T(8,128)(2,1)S(1)}, u32[]{:S(2)}, u32[]{:S(2)}) collective-permute-start(bf16[2,1024,256]{2,1,0:T(8,128)(2,1)S(1)} %collective-permute-done.3.refs_0_.refs_2_.refs_4_), channel_id=1, source_target_pairs={{0,2},{1,3},{2,4},{3,5},{4,6},{5,7},{6,0},{7,1},{8,10},{9,11},{10,... | collective-permute-start | bytes 3145736 | tf_op jit(solution)/shard_map/ppermute | solution.py:208
  137.8 31.3 %copy-start.21 = (bf16[2,1024,256]{2,1,0:T(8,128)(2,1)}, bf16[2,1024,256]{2,1,0:T(8,128)(2,1)S(1)}, u32[]{:S(2)}) copy-start(bf16[2,1024,256]{2,1,0:T(8,128)(2,1)S(1)} %collective-permute-done.5.refs_2_) | copy-start | bytes 3145732
  137.8 22.1 %collective-permute-start.29 = (bf16[2,1024,256]{2,1,0:T(8,128)(2,1)S(1)}, bf16[2,1024,256]{2,1,0:T(8,128)(2,1)S(1)}, u32[]{:S(2)}, u32[]{:S(2)}) collective-permute-start(bf16[2,1024,256]{2,1,0:T(8,128)(2,1)S(1)} %collective-permute-done.28.refs_8_), channel_id=1, source_target_pairs={{16,24},{17,25},{26,18},{27,19},{4,12},{5,13},{14,6},{15,7}} | collective-permute-start | bytes 3145736 | tf_op jit(solution)/shard_map/ppermute | solution.py:216
  138.5 30.6 %copy-start.13 = (bf16[2,1024,256]{2,1,0:T(8,128)(2,1)}, bf16[2,1024,256]{2,1,0:T(8,128)(2,1)S(1)}, u32[]{:S(2)}) copy-start(bf16[2,1024,256]{2,1,0:T(8,128)(2,1)S(1)} %collective-permute-done.25.refs_5_) | copy-start | bytes 3145732
  138.5 26.0 %collective-permute-start.18 = (bf16[2,1024,256]{2,1,0:T(8,128)(2,1)S(1)}, bf16[2,1024,256]{2,1,0:T(8,128)(2,1)}, u32[]{:S(2)}, u32[]{:S(2)}) collective-permute-start(bf16[2,1024,256]{2,1,0:T(8,128)(2,1)S(1)} %collective-permute-done.5.refs_2_), channel_id=1, source_target_pairs={{0,1},{1,0},{2,3},{3,2},{4,5},{5,4},{6,7},{7,6},{8,9},{9,8},{10,11... | collective-permute-start | bytes 3145736 | tf_op jit(solution)/shard_map/ppermute | solution.py:211
  139.7 27.1 %collective-permute-start.13 = (bf16[2,1024,256]{2,1,0:T(8,128)(2,1)S(1)}, bf16[2,1024,256]{2,1,0:T(8,128)(2,1)}, u32[]{:S(2)}, u32[]{:S(2)}) collective-permute-start(bf16[2,1024,256]{2,1,0:T(8,128)(2,1)S(1)} %collective-permute-done.11.refs_1_.refs_6_.refs_8_), channel_id=1, source_target_pairs={{0,16},{1,17},{10,26},{11,27},{20,4},{21,5},{30,14},{31,15}} | collective-permute-start | bytes 3145736 | tf_op jit(solution)/shard_map/ppermute | solution.py:214
  144.7 24.4 %copy-start.6 = (bf16[2,1024,256]{2,1,0:T(8,128)(2,1)}, bf16[2,1024,256]{2,1,0:T(8,128)(2,1)S(1)}, u32[]{:S(2)}) copy-start(bf16[2,1024,256]{2,1,0:T(8,128)(2,1)S(1)} %collective-permute-done.8.refs_3_.refs_5_) | copy-start | bytes 3145732
  144.7 24.3 %collective-permute-start.12 = (bf16[2,1024,256]{2,1,0:T(8,128)(2,1)S(1)}, bf16[2,1024,256]{2,1,0:T(8,128)(2,1)S(1)}, u32[]{:S(2)}, u32[]{:S(2)}) collective-permute-start(bf16[2,1024,256]{2,1,0:T(8,128)(2,1)S(1)} %collective-permute-done.11.refs_1_.refs_6_.refs_8_), channel_id=1, source_target_pairs={{0,8},{1,9},{10,2},{11,3},{20,28},{21,29},{30,22},{31,23}} | collective-permute-start | bytes 3145736 | tf_op jit(solution)/shard_map/ppermute | solution.py:215
  158.3 51.5 %copy-start.2 = (bf16[2,1024,256]{2,1,0:T(8,128)(2,1)}, bf16[2,1024,256]{2,1,0:T(8,128)(2,1)S(1)}, u32[]{:S(2)}) copy-start(bf16[2,1024,256]{2,1,0:T(8,128)(2,1)S(1)} %collective-permute-done.6.refs_0_.refs_2_.refs_12_) | copy-start | bytes 3145732
  158.3 33.0 %collective-permute-start.10 = (bf16[2,1024,256]{2,1,0:T(8,128)(2,1)}, bf16[2,1024,256]{2,1,0:T(8,128)(2,1)}, u32[]{:S(2)}, u32[]{:S(2)}) collective-permute-start(bf16[2,1024,256]{2,1,0:T(8,128)(2,1)} %collective-permute-done.9.refs_4_.refs_6_), channel_id=1, source_target_pairs={{16,24},{17,25},{26,18},{27,19},{4,12},{5,13},{14,6},{15,7}} | collective-permute-start | bytes 3145736 | tf_op jit(solution)/shard_map/ppermute | solution.py:216
  159.9 9.2 %copy-start.14 = (bf16[2,1024,256]{2,1,0:T(8,128)(2,1)}, bf16[2,1024,256]{2,1,0:T(8,128)(2,1)S(1)}, u32[]{:S(2)}) copy-start(bf16[2,1024,256]{2,1,0:T(8,128)(2,1)S(1)} %collective-permute-done.29.refs_9_) | copy-start | bytes 3145732
  159.9 32.7 %collective-permute-start.16 = (bf16[2,1024,256]{2,1,0:T(8,128)(2,1)S(1)}, bf16[2,1024,256]{2,1,0:T(8,128)(2,1)}, u32[]{:S(2)}, u32[]{:S(2)}) collective-permute-start(bf16[2,1024,256]{2,1,0:T(8,128)(2,1)S(1)} %collective-permute-done.6.refs_0_.refs_2_.refs_12_), channel_id=1, source_target_pairs={{0,16},{1,17},{10,26},{11,27},{20,4},{21,5},{30,14},{31,15}} | collective-permute-start | bytes 3145736 | tf_op jit(solution)/shard_map/ppermute | solution.py:214
  164.5 29.8 %collective-permute-start.20 = (bf16[2,1024,256]{2,1,0:T(8,128)(2,1)}, bf16[2,1024,256]{2,1,0:T(8,128)(2,1)}, u32[]{:S(2)}, u32[]{:S(2)}) collective-permute-start(bf16[2,1024,256]{2,1,0:T(8,128)(2,1)} %collective-permute-done.18.refs_1_.refs_6_.refs_16_), channel_id=1, source_target_pairs={{0,16},{1,17},{10,26},{11,27},{20,4},{21,5},{30,14},{31,15}} | collective-permute-start | bytes 3145736 | tf_op jit(solution)/shard_map/ppermute | solution.py:214
  166.8 41.3 %collective-permute-start.15 = (bf16[2,1024,256]{2,1,0:T(8,128)(2,1)S(1)}, bf16[2,1024,256]{2,1,0:T(8,128)(2,1)}, u32[]{:S(2)}, u32[]{:S(2)}) collective-permute-start(bf16[2,1024,256]{2,1,0:T(8,128)(2,1)S(1)} %collective-permute-done.6.refs_0_.refs_2_.refs_12_), channel_id=1, source_target_pairs={{0,8},{1,9},{10,2},{11,3},{20,28},{21,29},{30,22},{31,23}} | collective-permute-start | bytes 3145736 | tf_op jit(solution)/shard_map/ppermute | solution.py:215
  169.1 1.0 copy-start.7
  170.1 39.6 %collective-permute-start.14 = (bf16[2,1024,256]{2,1,0:T(8,128)(2,1)}, bf16[2,1024,256]{2,1,0:T(8,128)(2,1)}, u32[]{:S(2)}, u32[]{:S(2)}) collective-permute-start(bf16[2,1024,256]{2,1,0:T(8,128)(2,1)} %collective-permute-done.13.refs_8_.refs_10_), channel_id=1, source_target_pairs={{16,24},{17,25},{26,18},{27,19},{4,12},{5,13},{14,6},{15,7}} | collective-permute-start | bytes 3145736 | tf_op jit(solution)/shard_map/ppermute | solution.py:216
  191.3 43.4 %collective-permute-start.19 = (bf16[2,1024,256]{2,1,0:T(8,128)(2,1)}, bf16[2,1024,256]{2,1,0:T(8,128)(2,1)S(1)}, u32[]{:S(2)}, u32[]{:S(2)}) collective-permute-start(bf16[2,1024,256]{2,1,0:T(8,128)(2,1)} %collective-permute-done.18.refs_1_.refs_6_.refs_16_), channel_id=1, source_target_pairs={{0,8},{1,9},{10,2},{11,3},{20,28},{21,29},{30,22},{31,23}} | collective-permute-start | bytes 3145736 | tf_op jit(solution)/shard_map/ppermute | solution.py:215
  192.7 42.0 %collective-permute-start.17 = (bf16[2,1024,256]{2,1,0:T(8,128)(2,1)}, bf16[2,1024,256]{2,1,0:T(8,128)(2,1)}, u32[]{:S(2)}, u32[]{:S(2)}) collective-permute-start(bf16[2,1024,256]{2,1,0:T(8,128)(2,1)} %collective-permute-done.16.refs_4_.refs_14_), channel_id=1, source_target_pairs={{16,24},{17,25},{26,18},{27,19},{4,12},{5,13},{14,6},{15,7}} | collective-permute-start | bytes 3145736 | tf_op jit(solution)/shard_map/ppermute | solution.py:216
  194.4 40.3 %collective-permute-start.21 = (bf16[2,1024,256]{2,1,0:T(8,128)(2,1)}, bf16[2,1024,256]{2,1,0:T(8,128)(2,1)}, u32[]{:S(2)}, u32[]{:S(2)}) collective-permute-start(bf16[2,1024,256]{2,1,0:T(8,128)(2,1)} %collective-permute-done.20.refs_8_.refs_18_), channel_id=1, source_target_pairs={{16,24},{17,25},{26,18},{27,19},{4,12},{5,13},{14,6},{15,7}} | collective-permute-start | bytes 3145736 | tf_op jit(solution)/shard_map/ppermute | solution.py:216
  208.1 41.5 %collective-permute-start.4 = (bf16[2,1024,256]{2,1,0:T(8,128)(2,1)S(1)}, bf16[2,1024,256]{2,1,0:T(8,128)(2,1)}, u32[]{:S(2)}, u32[]{:S(2)}) collective-permute-start(bf16[2,1024,256]{2,1,0:T(8,128)(2,1)S(1)} %collective-permute-done.3.refs_0_.refs_2_.refs_4_), channel_id=1, source_target_pairs={{0,1},{1,0},{2,3},{3,2},{4,5},{5,4},{6,7},{7,6},{8,9},{9,8},{10,11... | collective-permute-start | bytes 3145736 | tf_op jit(solution)/shard_map/ppermute | solution.py:211
  209.8 39.8 %collective-permute-start.7 = (bf16[2,1024,256]{2,1,0:T(8,128)(2,1)S(1)}, bf16[2,1024,256]{2,1,0:T(8,128)(2,1)}, u32[]{:S(2)}, u32[]{:S(2)}) collective-permute-start(bf16[2,1024,256]{2,1,0:T(8,128)(2,1)S(1)} %collective-permute-done.6.refs_0_.refs_2_.refs_12_), channel_id=1, source_target_pairs={{0,1},{1,0},{2,3},{3,2},{4,5},{5,4},{6,7},{7,6},{8,9},{9,8},{10,11... | collective-permute-start | bytes 3145736 | tf_op jit(solution)/shard_map/ppermute | solution.py:211
  234.7 1.0 copy-start.8
